TPU v7x, 128 devices: a whole 4x4x4 slice. The times are simulated.
128 devices in a mesh: dp: 32 (over z_lo, y, x), mp: 4 (over z_hi, core).
Axes of the slice: x: 4, y: 4, z: 4 (z_hi: 2, z_lo: 2; z = z_hi * 2 + z_lo), core: 2. Of those that a mesh axis runs over, the one named last changes fastest.
Arguments:
- queries: bfloat16 [20480, 4096], P('dp', 'mp'), may hold values from -180 to 180
- keys: bfloat16 [20480, 512], P('dp', 'mp'), may hold values from -6 to 6
- values: bfloat16 [20480, 512], P('dp', 'mp'), may hold values from -6 to 6
- prompt_keys: bfloat16 [128, 512], P(None, 'mp'), may hold values from -6 to 6
- prompt_values: bfloat16 [128, 512], P(None, 'mp'), may hold values from -6 to 6
- out_weight: bfloat16 [4096, 8192], P('mp', 'dp'), may hold values from -0.09375 to 0.09375
- out_grad: bfloat16 [20480, 8192], P('dp'), may hold values from -6 to 6
- lengths: int32 [32, 8], P('dp'), may hold values from 1 to 320, 640 in all within a row
Outputs:
- mixed: bfloat16 [20480, 8192], P('dp', 'mp')
- prompt_key_grad: float32 [128, 512], P('dp', 'mp')
- prompt_value_grad: float32 [128, 512], P('dp', 'mp')
All inputs are finite; a program needn't handle non-finite values.
Results may differ from a plain program's by a relative error of at most 0.024.
Values may be sent and summed in bfloat16 or wider, within the bound.
A program may use at most 192 MiB of HBM per device.

v0:
```python
import jax
import jax.numpy as jnp
from jax import lax
from jax.sharding import PartitionSpec as P

HD = 128
rope_base = 1000000.0


def split_up(x, dim, length):
    dims = x.shape
    parts = x.reshape(*dims[:dim], length, dims[dim] // length, *dims[dim + 1 :])
    return jnp.moveaxis(parts, dim, 0)


def sum_at_owner(x, axis, dim):
    length = lax.axis_size(axis)
    parts = lax.all_to_all(split_up(x, dim, length), axis, 0, 0, tiled=True)
    return jnp.sum(parts.astype(jnp.float32), axis=0)


def sent_together(arrays, axis, dim, along):
    both = jnp.concatenate(arrays, axis=along)
    filled, at, finished = (sum_at_owner(both, axis, dim), 0, [])
    for a in arrays:
        finished.append(lax.slice_in_dim(filled, at, at + a.shape[along], axis=along))
        at += a.shape[along]
    return tuple(finished)


def doc_layout(lens, count):
    ends = jnp.cumsum(lens)
    starts = ends - lens
    index = jnp.arange(count, dtype=jnp.int32)
    segment = jnp.sum((index[:, None] >= ends[None, :]).astype(jnp.int32), axis=1)
    doc_ids = jnp.arange(lens.shape[0], dtype=jnp.int32)
    offset = jnp.sum(jnp.where(segment[:, None] == doc_ids[None, :], starts[None, :], 0), axis=1)
    return (segment, index - offset)


def rotate(field, position):
    half = HD // 2
    freq = rope_base ** (-2.0 * jnp.arange(half, dtype=jnp.float32) / HD)
    angle = position.astype(jnp.float32)[:, None] * freq[None, :]
    cosine = jnp.cos(angle)[:, None, :]
    sine = jnp.sin(angle)[:, None, :]
    first = field[..., :half].astype(jnp.float32)
    second = field[..., half:].astype(jnp.float32)
    return jnp.concatenate(
        [first * cosine - second * sine, second * cosine + first * sine], axis=-1
    ).astype(jnp.bfloat16)


def per_device(queries, keys, values, prompt_keys, prompt_values, out_weight, out_grad, lengths):
    tok_rows = queries.shape[0]
    kv_local = keys.shape[1] // HD
    groups = queries.shape[1] // HD // kv_local
    prompt_rows = prompt_keys.shape[0]
    scale = HD ** (-0.5)
    segment, position = doc_layout(lengths[0], tok_rows)
    q_rot = rotate(queries.reshape(tok_rows, kv_local * groups, HD), position).reshape(
        tok_rows, kv_local, groups, HD
    )
    k_rot = rotate(keys.reshape(tok_rows, kv_local, HD), position)
    key_all = jnp.concatenate([prompt_keys.reshape(prompt_rows, kv_local, HD), k_rot], axis=0)
    value_all = jnp.concatenate(
        [prompt_values.reshape(prompt_rows, kv_local, HD), values.reshape(tok_rows, kv_local, HD)],
        axis=0,
    )
    index = jnp.arange(tok_rows, dtype=jnp.int32)
    own = (segment[:, None] == segment[None, :]) & (index[None, :] <= index[:, None])
    key_mask = jnp.concatenate([jnp.ones((tok_rows, prompt_rows), dtype=bool), own], axis=1)
    scores = (
        jnp.einsum("tkgd,skd->kgts", q_rot, key_all, preferred_element_type=jnp.float32) * scale
    )
    scores = jnp.where(key_mask[None, None], scores, -1e30)
    shifted = jnp.exp(scores - jnp.max(scores, axis=-1, keepdims=True))
    shifted = jnp.where(key_mask[None, None], shifted, 0.0)
    probs = shifted / jnp.sum(shifted, axis=-1, keepdims=True)
    probs_b = probs.astype(jnp.bfloat16)
    attn = jnp.einsum("kgts,skd->tkgd", probs_b, value_all, preferred_element_type=jnp.float32)
    attn = attn.astype(jnp.bfloat16).reshape(tok_rows, kv_local * groups * HD)
    partial_value = jnp.dot(
        attn,
        lax.all_gather(out_weight, "dp", axis=1, tiled=True),
        preferred_element_type=jnp.float32,
    )
    grad_total = lax.dot_general(
        out_grad,
        lax.all_gather(out_weight, "dp", axis=1, tiled=True),
        (((1,), (1,)), ((), ())),
        preferred_element_type=jnp.float32,
    )
    mixed = lax.psum_scatter(
        partial_value.astype(jnp.bfloat16), "mp", scatter_dimension=1, tiled=True
    )
    grad_attn = grad_total.astype(jnp.bfloat16).reshape(tok_rows, kv_local, groups, HD)
    value_grad = jnp.einsum(
        "kgts,tkgd->skd", probs_b[..., :prompt_rows], grad_attn, preferred_element_type=jnp.float32
    )
    grad_probs = jnp.einsum(
        "tkgd,skd->kgts", grad_attn, value_all, preferred_element_type=jnp.float32
    )
    d_scores = probs * (grad_probs - jnp.sum(probs * grad_probs, axis=-1, keepdims=True)) * scale
    d_scores = d_scores.astype(jnp.bfloat16)
    key_grad = jnp.einsum(
        "kgts,tkgd->skd", d_scores[..., :prompt_rows], q_rot, preferred_element_type=jnp.float32
    )
    owned = sent_together(
        (
            key_grad.reshape(prompt_rows, kv_local * HD).astype(jnp.bfloat16),
            value_grad.reshape(prompt_rows, kv_local * HD).astype(jnp.bfloat16),
        ),
        "dp",
        0,
        1,
    )
    return (mixed, owned[0], owned[1])


def solution(mesh):
    in_specs = (
        P("dp", "mp"),
        P("dp", "mp"),
        P("dp", "mp"),
        P(None, "mp"),
        P(None, "mp"),
        P("mp", "dp"),
        P("dp", None),
        P("dp", None),
    )
    out_specs = (P("dp", "mp"), P("dp", "mp"), P("dp", "mp"))
    return jax.shard_map(
        per_device, mesh=mesh, in_specs=in_specs, out_specs=out_specs, check_vma=False
    )
```

profile of v0, /device:TPU:1, one launch (start us, length us, event | category | flops | bytes accessed | tf_op | source)
XLA Modules:
  0.0 424.6 jit_solution(10789679038603178659)
XLA Ops:
  7.2 0.0 all-gather.2.cloned.1.call-start
  7.2 0.7 all-gather.2.cloned.1.call-update
  7.9 0.0 reduce-scatter.2.cloned.1.call-start
  7.9 1.7 copy.39
  9.7 0.1 fusion.47
  9.8 0.0 copy-start.2
  9.8 0.0 copy-start.4
  9.8 0.0 copy-start.3
  9.8 0.0 copy-start.5
  9.8 0.0 copy-start.6
  9.8 1.4 copy.52
  11.3 1.4 copy.53
  12.7 0.0 copy-done.2
  12.7 0.2 copy.38
  12.9 0.0 copy-done.4
  12.9 0.1 copy.37
  13.0 0.0 copy-done.3
  13.0 0.2 copy.36
  13.2 0.1 copy.35
  13.3 0.0 copy-done.6
  13.3 0.2 reduce-window.4
  13.5 0.1 convert_reduce_fusion.1
  13.6 0.3 fusion.11
  13.8 0.1 concatenate.33
  13.9 0.1 select_reduce_fusion
  14.0 0.7 fusion.37
  14.8 1.2 multiply_cosine_fusion
  16.0 0.0 copy-done.1
  16.0 2.2 fusion.6
  18.1 7.5 %fusion = (f32[8,640]{1,0:T(8,128)S(1)}, f32[768,640,8]{1,0,2:T(8,128)}) fusion(pred[640,768]{0,1:T(8,128)(4,1)S(1)} %concatenate.33, bf16[640,8,64]{2,0,1:T(8,128)(2,1)S(1)} %get-tuple-element.6, bf16[640,8,64]{2,0,1:T(8,128)(2,1)S(1)} %get-tuple-element.5, bf16[640,1,64]{0,2,1:T(8,128)(2,1)S(1)} %get-tuple-element.10, ...), kind=kOutput, calls=%fused_computation.3 | convolution fusion | flops 1021635584 | bytes 17747968 | tf_op jit(solution)/shard_map/tkgd,skd->kgts/dot_general | solution.py:74
  25.7 9.3 %fusion.2 = f32[8,640]{1,0:T(8,128)S(1)} fusion(f32[768,640,8]{1,0,2:T(8,128)} %get-tuple-element.16, f32[8,640]{1,0:T(8,128)S(1)} %get-tuple-element.15, pred[640,768]{0,1:T(8,128)(4,1)S(1)} %concatenate.33), kind=kLoop, calls=%fused_computation.6 | loop fusion | flops 19655680 | bytes 16261120 | tf_op jit(solution)/shard_map/reduce_sum | solution.py:79
  35.0 203.2 %all-gather.2.cloned.1.call-done = bf16[1024,8192]{1,0:T(8,128)(2,1)} async-done(((bf16[1024,256]{1,0:T(8,128)(2,1)}), bf16[1024,8192]{1,0:T(8,128)(2,1)}) %all-gather.2.cloned.1.call-update) | async-done | bytes 16777232 | tf_op jit(solution)/shard_map/all_gather | solution.py:85
  238.2 17.4 %convolution_convert_fusion.1 = bf16[640,1024]{1,0:T(8,128)(2,1)} fusion(bf16[640,8192]{1,0:T(8,128)(2,1)} %param.14, bf16[1024,8192]{1,0:T(8,128)(2,1)} %all-gather.2.cloned.1.call-done), kind=kOutput, calls=%fused_computation.25 | convolution fusion | flops 10738073600 | bytes 28573696 | tf_op jit(solution)/shard_map/dot_general | solution.py:88
  255.6 17.4 %multiply_reduce_fusion = (f32[8,640]{1,0:T(8,128)S(1)}, f32[1,8,640,768]{2,3,1,0:T(8,128)}, f32[1,8,640,768]{2,3,1,0:T(8,128)}) fusion(f32[8,640]{1,0:T(8,128)S(1)} %fusion.2, f32[8,640]{1,0:T(8,128)S(1)} %get-tuple-element.15, f32[768,640,8]{1,0,2:T(8,128)} %get-tuple-element.16, pred[640,768]{0,1:T(8,128)(4,1)S(1)} %concatenate.33, ...), kind=kOutput, calls=%fused_computation.1 | convolution fusion | flops 1034546176 | bytes 49246208 | tf_op jit(solution)/shard_map/tkgd,skd->kgts/dot_general | solution.py:101
  273.0 9.4 %convert_element_type.92 = bf16[1,8,640,768]{2,3,1,0:T(8,128)(2,1)} convert(f32[1,8,640,768]{2,3,1,0:T(8,128)} %get-tuple-element.4) | non-fusion elementwise | flops 3932160 | bytes 23592960 | tf_op jit(solution)/shard_map/convert_element_type | solution.py:80
  282.4 4.4 %fusion.12 = bf16[128,8,640]{2,0,1:T(8,128)(2,1)S(1)} fusion(bf16[1,8,640,768]{2,3,1,0:T(8,128)(2,1)} %convert_element_type.92, bf16[640,1,128]{0,2,1:T(8,128)(2,1)S(1)} %bitcast.106, bf16[128,1,128]{0,2,1:T(8,128)(2,1)S(1)} %bitcast.108), kind=kOutput, calls=%fused_computation.24 | convolution fusion | flops 1007681536 | bytes 9371648 | tf_op jit(solution)/shard_map/kgts,skd->tkgd/dot_general | solution.py:81
  286.8 19.5 %convolution_convert_fusion = bf16[640,8192]{1,0:T(8,128)(2,1)} fusion(bf16[640,1024]{0,1:T(8,128)(2,1)S(1)} %bitcast.102, bf16[1024,8192]{1,0:T(8,128)(2,1)} %all-gather.2.cloned.1.call-done), kind=kOutput, calls=%fused_computation.4 | convolution fusion | flops 10742661120 | bytes 28573696 | tf_op jit(solution)/shard_map/dot_general | solution.py:83
  306.4 0.0 reduce-scatter.2.cloned.1.call-update
  306.4 2.5 slice_bitcast_fusion
  308.9 2.8 copy.46
  311.7 1.8 copy.55
  313.5 0.0 copy-done
  313.5 0.6 fusion.23
  314.1 3.7 fusion.24
  317.8 14.4 %all_to_all.5 = bf16[32,4,256]{2,1,0:T(4,128)(2,1)S(1)} all-to-all(bf16[32,4,256]{2,1,0:T(4,128)(2,1)S(1)} %pad_maximum_fusion.3), channel_id=1, replica_groups=mesh['dp'=32,'mp'=4] {'dp'}, dimensions={0} | all-to-all | bytes 131072 | tf_op jit(solution)/shard_map/all_to_all | solution.py:18
  332.2 0.1 convert_reduce_fusion
  332.3 0.6 fusion.48
  332.9 84.9 %reduce-scatter.2.cloned.1.call-done = bf16[640,2048]{1,0:T(8,128)(2,1)} async-done(((bf16[640,8192]{1,0:T(8,128)(2,1)}), bf16[640,2048]{1,0:T(8,128)(2,1)}) %reduce-scatter.2.cloned.1.call-update) | async-done | bytes 2621456 | tf_op jit(solution)/shard_map/reduce_scatter | solution.py:94
  (7 shorter events, 0.1 us)
Async XLA Ops:
  7.2 231.0 %all-gather.2.cloned.1.call-start = ((), (), s32[]{:S(2)}) async-start(), calls=%async_computation.2 | async-start | bytes 17301504 | tf_op jit(solution)/shard_map/all_gather | solution.py:85
  7.9 409.9 %reduce-scatter.2.cloned.1.call-start = ((), (), s32[]{:S(2)}) async-start(), calls=%async_computation.3 | async-start | bytes 13107200 | tf_op jit(solution)/shard_map/reduce_scatter | solution.py:94
  9.8 2.9 copy-start.2
  9.8 3.1 copy-start.4
  9.8 3.2 copy-start.3
  9.8 3.3 copy-start.5
  9.8 3.4 copy-start.6
  13.5 2.5 copy-start.1
  311.7 1.8 copy-start
Sparse Core Ops, SparseCore 0:
  9.6 228.5 all-gather.1
  306.5 111.1 reduce-scatter.1
where the time goes:
time: 425 us
  waiting for transfers between devices  289 us (68%)
  matrix products  70.5 us (17%)
  other arithmetic  23.5 us (6%)
  blocking collectives  14.4 us (3%)
  between operations  14.3 us (3%)
  local copies, waits for them, and re-layouts  13 us (3%)
    all_gather x1, waiting for transfers between devices, per_device(): lax.all_gather(out_weight, 'dp', axis=1, tiled=True)  203 us
    reduce_scatter x1, waiting for transfers between devices, per_device(): lax.psum_scatter(partial_value.astype(jnp.bfloat16), 'mp', scatter_dimens...  84.9 us
    dot_general x1, matrix products, per_device(): jnp.dot(attn, lax.all_gather(out_weight, 'dp', axis=1, tiled=True), prefe...  19.5 us
    dot_general x1, matrix products, per_device(): lax.dot_general(out_grad, lax.all_gather(out_weight, 'dp', axis=1, tiled=...  17.4 us
    dot_general x1, matrix products, per_device(): jnp.einsum('tkgd,skd->kgts', grad_attn, value_all, preferred_element_type...  17.4 us
    all_to_all x1, blocking collectives, sum_at_owner(): parts = lax.all_to_all(split_up(x, dim, length), axis, 0, 0, tiled=True)  14.4 us
    convert_element_type x1, other arithmetic, per_device(): probs_b = probs.astype(jnp.bfloat16)  9.41 us
    reduce_sum x1, other arithmetic, per_device(): probs = shifted / jnp.sum(shifted, axis=-1, keepdims=True)  9.28 us
  transfers between devices with their start and end apart: 2, of which 2 were waited for; matrix products, arithmetic and copies ran while one was open for 9% of the time, Pallas kernels for 0%

commit v1 on v0

--- a/solution.py
+++ b/solution.py
@@ -82,7 +82,9 @@
     attn = attn.astype(jnp.bfloat16).reshape(tok_rows, kv_local * groups * HD)
     partial_value = jnp.dot(
         attn,
-        lax.all_gather(out_weight, "dp", axis=1, tiled=True),
+        jnp.concatenate(
+            lax.all_to_all(jnp.stack([out_weight] * lax.axis_size("dp")), "dp", 0, 0), axis=1
+        ),
         preferred_element_type=jnp.float32,
     )
     grad_total = lax.dot_general(

time: 425 us -> 634 us (1.49)
  waiting for transfers between devices: 289 us -> 481 us
  starting transfers between devices: 0.08 us -> 9.56 us
  local copies, waits for them, and re-layouts: 13 us -> 19.4 us
    all_gather x1, waiting for transfers between devices: 203 us -> 400 us  [per_device(): lax.all_gather(out_weight, 'dp', axis=1, tiled=True)]
    all_to_all x0 -> x1, starting transfers between devices: none -> 9.48 us  [per_device(): lax.all_to_all(jnp.stack([out_weight] * lax.axis_size('dp')), 'dp', 0, 0)]
  transfers between devices with their start and end apart: 2 -> 3, of which waited for: 2 -> 2; matrix products, arithmetic and copies ran while one was open for 9% -> 15% of each run, Pallas kernels for 0% -> 0%
where the time goes in v1:
time: 634 us; the launch traced here: 633 us
  waiting for transfers between devices  481 us (76%)
  matrix products  69.4 us (11%)
  other arithmetic  23.5 us (4%)
  local copies, waits for them, and re-layouts  19.4 us (3%)
  blocking collectives  16 us (3%)
  between operations  14.3 us (2%)
  starting transfers between devices  9.56 us (2%)
    all_gather x1, waiting for transfers between devices, per_device(): lax.all_gather(out_weight, 'dp', axis=1, tiled=True)  400 us
    reduce_scatter x1, waiting for transfers between devices, per_device(): lax.psum_scatter(partial_value.astype(jnp.bfloat16), 'mp', scatter_dimens...  80.6 us
    dot_general x1, matrix products, per_device(): lax.dot_general(out_grad, lax.all_gather(out_weight, 'dp', axis=1, tiled=...  17.4 us
    dot_general x1, matrix products, per_device(): jnp.dot(attn, jnp.concatenate(lax.all_to_all(jnp.stack([out_weight] * lax...  17.3 us
    dot_general x1, matrix products, per_device(): jnp.einsum('tkgd,skd->kgts', grad_attn, value_all, preferred_element_type...  17.3 us
    all_to_all x1, blocking collectives, sum_at_owner(): parts = lax.all_to_all(split_up(x, dim, length), axis, 0, 0, tiled=True)  16 us
  transfers between devices with their start and end apart: 3, of which 2 were waited for; matrix products, arithmetic and copies ran while one was open for 15% of the time, Pallas kernels for 0%

profile of v1, /device:TPU:1, one launch (start us, length us, event | category | flops | bytes accessed | tf_op | source)
XLA Modules:
  0.0 633.3 jit_solution(18145994821524665523)
XLA Ops:
  7.2 0.0 all-gather.2.cloned.1.call-start
  7.2 0.7 all-gather.2.cloned.1.call-update
  7.9 1.2 copy.46
  9.2 6.0 stack.2
  15.1 9.5 %all-to-all-start = ((bf16[32,1024,256]{1,2,0:T(8,128)(2,1)}), bf16[32,1024,256]{1,2,0:T(8,128)(2,1)}, u32[]{:S(2)}, u32[]{:S(2)}) async-start(bf16[32,1024,256]{1,2,0:T(8,128)(2,1)} %stack.2), calls=%async_computation | async-start | bytes 33554432 | tf_op jit(solution)/shard_map/all_to_all | solution.py:86
  24.6 0.0 reduce-scatter.2.cloned.1.call-start
  24.7 0.7 copy.41
  25.4 0.1 fusion.47
  25.6 0.0 copy-start.3
  25.6 0.0 copy-start.5
  25.6 0.0 copy-start.4
  25.6 0.0 copy-start.6
  25.6 0.0 copy-start.7
  25.6 1.4 copy.55
  27.0 1.4 copy.56
  28.5 0.2 copy.40
  28.6 0.0 copy-done.5
  28.7 0.1 copy.39
  28.8 0.0 copy-done.4
  28.8 0.2 copy.38
  29.0 0.1 copy.37
  29.1 0.2 reduce-window.4
  29.3 0.1 convert_reduce_fusion.1
  29.4 0.3 fusion.11
  29.6 0.1 concatenate.33
  29.7 0.1 select_reduce_fusion
  29.8 0.7 fusion.37
  30.5 1.2 multiply_cosine_fusion
  31.8 2.2 fusion.6
  33.9 7.6 %fusion = (f32[8,640]{1,0:T(8,128)S(1)}, f32[768,640,8]{1,0,2:T(8,128)}) fusion(pred[640,768]{0,1:T(8,128)(4,1)S(1)} %concatenate.33, bf16[640,8,64]{2,0,1:T(8,128)(2,1)S(1)} %get-tuple-element.6, bf16[640,8,64]{2,0,1:T(8,128)(2,1)S(1)} %get-tuple-element.5, bf16[640,1,64]{0,2,1:T(8,128)(2,1)S(1)} %get-tuple-element.10, ...), kind=kOutput, calls=%fused_computation.3 | convolution fusion | flops 1021635584 | bytes 17747968 | tf_op jit(solution)/shard_map/tkgd,skd->kgts/dot_general | solution.py:74
  41.6 9.3 %fusion.2 = f32[8,640]{1,0:T(8,128)S(1)} fusion(f32[768,640,8]{1,0,2:T(8,128)} %get-tuple-element.16, f32[8,640]{1,0:T(8,128)S(1)} %get-tuple-element.15, pred[640,768]{0,1:T(8,128)(4,1)S(1)} %concatenate.33), kind=kLoop, calls=%fused_computation.6 | loop fusion | flops 19655680 | bytes 16261120 | tf_op jit(solution)/shard_map/reduce_sum | solution.py:79
  50.8 399.8 %all-gather.2.cloned.1.call-done = bf16[1024,8192]{1,0:T(8,128)(2,1)} async-done(((bf16[1024,256]{1,0:T(8,128)(2,1)}), bf16[1024,8192]{1,0:T(8,128)(2,1)}) %all-gather.2.cloned.1.call-update) | async-done | bytes 16777232 | tf_op jit(solution)/shard_map/all_gather | solution.py:92
  450.7 17.4 %convolution_convert_fusion.1 = bf16[640,1024]{1,0:T(8,128)(2,1)} fusion(bf16[640,8192]{1,0:T(8,128)(2,1)} %param.14, bf16[1024,8192]{1,0:T(8,128)(2,1)} %all-gather.2.cloned.1.call-done), kind=kOutput, calls=%fused_computation.25 | convolution fusion | flops 10738073600 | bytes 28573696 | tf_op jit(solution)/shard_map/dot_general | solution.py:90
  468.1 17.3 %multiply_reduce_fusion = (f32[8,640]{1,0:T(8,128)S(1)}, f32[1,8,640,768]{2,3,1,0:T(8,128)}, f32[1,8,640,768]{2,3,1,0:T(8,128)}) fusion(f32[8,640]{1,0:T(8,128)S(1)} %fusion.2, f32[8,640]{1,0:T(8,128)S(1)} %get-tuple-element.15, f32[768,640,8]{1,0,2:T(8,128)} %get-tuple-element.16, pred[640,768]{0,1:T(8,128)(4,1)S(1)} %concatenate.33, ...), kind=kOutput, calls=%fused_computation.1 | convolution fusion | flops 1034546176 | bytes 49246208 | tf_op jit(solution)/shard_map/tkgd,skd->kgts/dot_general | solution.py:103
  485.4 9.5 %convert_element_type.92 = bf16[1,8,640,768]{2,3,1,0:T(8,128)(2,1)} convert(f32[1,8,640,768]{2,3,1,0:T(8,128)} %get-tuple-element.4) | non-fusion elementwise | flops 3932160 | bytes 23592960 | tf_op jit(solution)/shard_map/convert_element_type | solution.py:80
  494.9 5.5 fusion.12
  500.4 0.0 all-to-all-done
  500.4 17.3 %convolution_convert_fusion = bf16[640,8192]{1,0:T(8,128)(2,1)} fusion(bf16[640,1024]{0,1:T(8,128)(2,1)} %bitcast.105, bf16[1024,8192]{0,1:T(8,128)(2,1)} %bitcast.20), kind=kOutput, calls=%fused_computation.4 | convolution fusion | flops 10742661120 | bytes 28573696 | tf_op jit(solution)/shard_map/dot_general | solution.py:83
  517.7 0.0 reduce-scatter.2.cloned.1.call-update
  517.7 2.5 slice_bitcast_fusion
  520.2 2.9 copy.49
  523.1 1.8 copy.58
  524.9 0.6 fusion.23
  525.5 3.7 fusion.24
  529.2 16.0 %all_to_all.10 = bf16[32,4,256]{2,1,0:T(4,128)(2,1)S(1)} all-to-all(bf16[32,4,256]{2,1,0:T(4,128)(2,1)S(1)} %pad_maximum_fusion.3), channel_id=1, replica_groups=mesh['dp'=32,'mp'=4] {'dp'}, dimensions={0} | all-to-all | bytes 131072 | tf_op jit(solution)/shard_map/all_to_all | solution.py:18
  545.2 0.1 convert_reduce_fusion
  545.3 0.6 fusion.48
  545.9 80.6 %reduce-scatter.2.cloned.1.call-done = bf16[640,2048]{1,0:T(8,128)(2,1)} async-done(((bf16[640,8192]{1,0:T(8,128)(2,1)}), bf16[640,2048]{1,0:T(8,128)(2,1)}) %reduce-scatter.2.cloned.1.call-update) | async-done | bytes 2621456 | tf_op jit(solution)/shard_map/reduce_scatter | solution.py:96
  (13 shorter events, 0.1 us)
Async XLA Ops:
  7.2 443.5 %all-gather.2.cloned.1.call-start = ((), (), s32[]{:S(2)}) async-start(), calls=%async_computation.4 | async-start | bytes 17301504 | tf_op jit(solution)/shard_map/all_gather | solution.py:92
  15.1 9.5 %copy-start.2 = (bf16[640,1024]{1,0:T(8,128)(2,1)S(1)}, bf16[640,1024]{1,0:T(8,128)(2,1)}, u32[]{:S(2)}) copy-start(bf16[640,1024]{1,0:T(8,128)(2,1)} %param.8) | copy-start | bytes 3932164
  15.1 485.2 %all-to-all-start = ((bf16[32,1024,256]{1,2,0:T(8,128)(2,1)}), bf16[32,1024,256]{1,2,0:T(8,128)(2,1)}, u32[]{:S(2)}, u32[]{:S(2)}) async-start(bf16[32,1024,256]{1,2,0:T(8,128)(2,1)} %stack.2), calls=%async_computation | async-start | bytes 33554432 | tf_op jit(solution)/shard_map/all_to_all | solution.py:86
  24.6 601.8 %reduce-scatter.2.cloned.1.call-start = ((), (), s32[]{:S(2)}) async-start(), calls=%async_computation.3 | async-start | bytes 13107200 | tf_op jit(solution)/shard_map/reduce_scatter | solution.py:96
  25.6 2.9 copy-start.3
  25.6 3.1 copy-start.5
  25.6 3.2 copy-start.4
  25.6 3.4 copy-start.6
  25.6 3.5 copy-start.7
  29.3 2.5 copy-start.1
  523.1 1.8 copy-start
Sparse Core Ops, SparseCore 0:
  9.6 441.0 all-gather.1
  517.8 108.5 reduce-scatter.1
